TPU v7x, 256 devices: a whole 4x4x8 slice. The times are simulated.
256 devices in a mesh: tok: 64 (over z, x, core), grp: 4 (over y).
Axes of the slice: x: 4, y: 4, z: 8, core: 2. Of those that a mesh axis runs over, the one named last changes fastest.
Arguments:
- inputs: float32 [4, 8192, 1536], P('grp', 'tok'), may hold values from -6 to 6
- queries: bfloat16 [4, 8192, 1536], P('grp', 'tok'), may hold values from -100 to 100
- keys: bfloat16 [4, 8192, 256], P('grp', 'tok'), may hold values from -6 to 6
- values: bfloat16 [4, 8192, 256], P('grp', 'tok'), may hold values from -6 to 6
- prefix_keys: bfloat16 [2048, 256], P(('tok', 'grp')), may hold values from -7 to 7
- prefix_values: bfloat16 [2048, 256], P(('tok', 'grp')), may hold values from -6 to 6
- lengths: int32 [4, 16], replicated, may hold values from 1 to 4224, 8192 in all within a row
- out_weight: bfloat16 [1536, 1536], replicated, may hold values from -0.5 to 0.5
- norm_gain: float32 [1536], replicated, may hold values from 0.25 to 1.75
- router_weight: bfloat16 [1536, 32], replicated, may hold values from -0.15625 to 0.15625
- routes: int32 [4, 8192, 4], P('grp', 'tok'), may hold values from 0 to 31, all different within a row; in each aligned block of 128 rows (0 to 127, 128 to 255, ..., all dimensions but the last counted through in order) at most 24 rows name the same one
- expert_gate: bfloat16 [64, 1536, 384], P('tok'), may hold values from -0.15625 to 0.15625
- expert_up: bfloat16 [64, 1536, 384], P('tok'), may hold values from -0.15625 to 0.15625
- expert_down: bfloat16 [64, 384, 1536], P('tok'), may hold values from -0.21875 to 0.21875
Outputs:
- layer_out: float32 [4, 8192, 1536], P('grp', 'tok')
Inputs may be any that keep to these rules, and one draw needn't show every extreme that they name: Row g holds the suffix lengths of the 16 requests of group g, in order; they sum to 8192, and the longest is exactly 4224. `routes`: each token names 4 different experts; of one device's 128 tokens no more than 24 name one expert, and in every draw some expert is named by exactly 24 of them.
All inputs are finite; a program needn't handle non-finite values.
Results may differ from a plain program's by a relative error of at most 0.0055.
Values may be sent and summed in bfloat16 or wider, within the bound.
A program may use at most 192 MiB of HBM per device.

v0:
```python
import math

import jax
import jax.numpy as jnp
from jax import lax
from jax.sharding import PartitionSpec as P

HEADS = 12
KVH = 2
HD = 128
EXPERTS = 32
TOP = 4
CAP = 24


NEGATIVE = -1e30


def absorb(running, key_piece, value_piece, valid, query_heads):
    running_max, denominator, numerator = running
    key_count = key_piece.shape[0]
    key_heads = key_piece.reshape(key_count, KVH, HD)
    value_heads = value_piece.reshape(key_count, KVH, HD)
    scores = jnp.einsum(
        "tgrd,kgd->grtk", query_heads, key_heads, preferred_element_type=jnp.float32
    ) * (1.0 / math.sqrt(HD))
    if valid is None:
        masked = scores
    else:
        masked = jnp.where(valid[None, None], scores, NEGATIVE)
    new_max = jnp.maximum(running_max, jnp.max(masked, axis=-1))
    factor = jnp.exp(running_max - new_max)
    weights = jnp.exp(masked - new_max[..., None])
    if valid is not None:
        weights = jnp.where(valid[None, None], weights, 0.0)
    denominator = denominator * factor + jnp.sum(weights, axis=-1)
    numerator = numerator * factor[..., None] + jnp.einsum(
        "grtk,kgd->grtd",
        weights.astype(jnp.bfloat16),
        value_heads,
        preferred_element_type=jnp.float32,
    )
    return (new_max, denominator, numerator)


def local(
    inputs,
    queries,
    keys,
    values,
    prefix_keys,
    prefix_values,
    lengths,
    out_weight,
    norm_gain,
    router_weight,
    routes,
    expert_gate,
    expert_up,
    expert_down,
):
    tok_rows = queries.shape[1]
    model_width = out_weight.shape[1]
    repeat = HEADS // KVH
    query_heads = queries[0].reshape(tok_rows, KVH, repeat, HD)
    device = lax.axis_index("tok")
    positions = device * tok_rows + jnp.arange(tok_rows, dtype=jnp.int32)
    row_lengths = lax.dynamic_index_in_dim(lengths, lax.axis_index("grp"), 0, keepdims=False)
    request_ends = jnp.cumsum(row_lengths)
    starts = jnp.max(
        jnp.where(request_ends[None, :] <= positions[:, None], request_ends[None, :], 0), axis=1
    )
    softmax_state = (
        jnp.full((KVH, repeat, tok_rows), NEGATIVE, jnp.float32),
        jnp.zeros((KVH, repeat, tok_rows), jnp.float32),
        jnp.zeros((KVH, repeat, tok_rows, HD), jnp.float32),
    )
    shard_pair = (
        lax.all_gather(prefix_keys, ("tok", "grp"), axis=0, tiled=True),
        lax.all_gather(prefix_values, ("tok", "grp"), axis=0, tiled=True),
    )
    softmax_state = absorb(softmax_state, shard_pair[0], shard_pair[1], None, query_heads)
    own_keys = keys[0]
    own_values = values[0]
    shard_pair = (
        lax.all_gather(own_keys, "tok", axis=0, tiled=True),
        lax.all_gather(own_values, "tok", axis=0, tiled=True),
    )
    key_positions = jnp.arange(shard_pair[0].shape[0], dtype=jnp.int32)
    softmax_state = absorb(
        softmax_state,
        shard_pair[0],
        shard_pair[1],
        (key_positions[None, :] >= starts[:, None])
        & (key_positions[None, :] <= positions[:, None]),
        query_heads,
    )
    attended = (softmax_state[2] / softmax_state[1][..., None]).astype(jnp.bfloat16)
    attended = attended.transpose(2, 0, 1, 3).reshape(tok_rows, HEADS * HD)
    residual = inputs[0] + jnp.dot(attended, out_weight, preferred_element_type=jnp.float32)
    normed = (
        residual
        * lax.rsqrt(jnp.mean(residual * residual, axis=-1, keepdims=True) + 1e-06)
        * norm_gain
    ).astype(jnp.bfloat16)
    logits = jnp.dot(normed, router_weight, preferred_element_type=jnp.float32)
    token_routes = routes[0]
    sigmoids = jax.nn.sigmoid(jnp.take_along_axis(logits, token_routes, axis=1))
    gate_weights = sigmoids / jnp.sum(sigmoids, axis=1, keepdims=True)
    pair_experts = token_routes.reshape(-1)
    onehot = (pair_experts[:, None] == jnp.arange(EXPERTS, dtype=jnp.int32)[None, :]).astype(
        jnp.int32
    )
    slot_index = jnp.sum(jnp.cumsum(onehot, axis=0) * onehot, axis=1) - 1
    targets = pair_experts * CAP + slot_index
    buffer = (
        jnp.zeros((EXPERTS * CAP, model_width), jnp.bfloat16)
        .at[targets]
        .set(jnp.repeat(normed, TOP, axis=0))
    )
    local_slices = expert_gate.shape[0]
    tok_count = lax.axis_size("tok")
    split_count = local_slices * tok_count // EXPERTS
    outgoing = jnp.repeat(buffer.reshape(EXPERTS, CAP, model_width), split_count, axis=0).reshape(
        tok_count, local_slices, CAP, model_width
    )
    weight_sets = (expert_gate[:, None], expert_up[:, None], expert_down[:, None])
    arrived = lax.all_to_all(outgoing, "tok", split_axis=0, concat_axis=0, tiled=True)
    sources = arrived.shape[0]
    slot_count = arrived.shape[2]
    slot_rows = arrived[:, 0].reshape(sources * slot_count, model_width)
    gated = jax.nn.relu(
        jnp.dot(slot_rows, weight_sets[0][0, 0], preferred_element_type=jnp.float32)
    )
    hidden = (
        gated * jnp.dot(slot_rows, weight_sets[1][0, 0], preferred_element_type=jnp.float32)
    ).astype(jnp.bfloat16)
    part_out = jnp.dot(hidden, weight_sets[2][0, 0], preferred_element_type=jnp.float32).astype(
        jnp.bfloat16
    )
    total = lax.optimization_barrier(part_out).astype(jnp.float32)
    results = [total.astype(jnp.bfloat16).reshape(sources, slot_count, model_width)]
    computed = jnp.stack(results, axis=1)
    returned = lax.all_to_all(computed, "tok", split_axis=0, concat_axis=0, tiled=True)
    summed = jnp.sum(
        returned.reshape(EXPERTS, split_count, CAP, model_width).astype(jnp.float32), axis=1
    ).reshape(EXPERTS * CAP, model_width)
    expert_out = lax.optimization_barrier(summed.astype(jnp.bfloat16)).astype(jnp.float32)
    combined = jnp.sum(
        expert_out[targets].reshape(tok_rows, TOP, model_width) * gate_weights[:, :, None], axis=1
    )
    return (residual + combined)[None]


def solution(mesh):
    placed = (
        P("grp", "tok", None),
        P("grp", "tok", None),
        P("grp", "tok", None),
        P("grp", "tok", None),
        P(("tok", "grp"), None),
        P(("tok", "grp"), None),
        P(),
        P(),
        P(),
        P(),
        P("grp", "tok", None),
        P("tok", None, None),
        P("tok", None, None),
        P("tok", None, None),
    )
    return jax.shard_map(
        local, mesh=mesh, in_specs=placed, out_specs=P("grp", "tok", None), check_vma=False
    )
```

profile of v0, /device:TPU:16, one launch (start us, length us, event | category | flops | bytes accessed | tf_op | source)
XLA Modules:
  0.0 691.6 jit_solution(8346470615721139849)
XLA Ops:
  17.6 99.2 %all-gather.7.cloned.1.call-done = bf16[2048,256]{1,0:T(8,128)(2,1)} async-done(((bf16[8,256]{1,0:T(8,128)(2,1)}), bf16[2048,256]{1,0:T(8,128)(2,1)}) %all-gather.7.cloned.1.call-update) | async-done | bytes 1048592 | tf_op jit(solution)/shard_map/all_gather | solution.py:79
  118.3 7.3 %bitcast_reduce_fusion = (f32[2,6,128]{2,1,0:T(8,128)S(1)}, f32[2,2048,128,6]{2,1,3,0:T(8,128)}) fusion(bf16[2048,2,128,1]{0,2,3,1:T(8,128)(2,1)S(1)} %bitcast.168, bf16[128,2,6,128]{0,3,2,1:T(8,128)(2,1)} %bitcast.171), kind=kOutput, calls=%fused_computation.11 | convolution fusion | flops 811596288 | bytes 14030848 | tf_op jit(solution)/shard_map/tgrd,kgd->grtk/dot_general | solution.py:24
  125.6 96.9 %all-gather.9.cloned.1.call-done = bf16[2048,256]{1,0:T(8,128)(2,1)} async-done(((bf16[8,256]{1,0:T(8,128)(2,1)}), bf16[2048,256]{1,0:T(8,128)(2,1)}) %all-gather.9.cloned.1.call-update) | async-done | bytes 1048592 | tf_op jit(solution)/shard_map/all_gather | solution.py:80
  224.0 76.4 %all-gather.11.cloned.1.call-done = bf16[1,8192,256]{1,2,0:T(8,128)(2,1)} async-done(((bf16[1,128,256]{1,2,0:T(8,128)(2,1)}), bf16[1,8192,256]{1,2,0:T(8,128)(2,1)}) %all-gather.11.cloned.1.call-update) | async-done | bytes 4194320 | tf_op jit(solution)/shard_map/all_gather | solution.py:86
  300.3 21.5 %fusion = (f32[2,6,128]{2,1,0:T(8,128)S(1)}, f32[2,8192,128,6]{2,1,3,0:T(8,128)}) fusion(pred[128,8192]{0,1:T(8,128)(4,1)S(1)} %fusion.11, bf16[8192,2,128,1]{0,2,3,1:T(8,128)(2,1)} %bitcast.177, bf16[128,2,6,128]{0,3,2,1:T(8,128)(2,1)} %bitcast.172), kind=kOutput, calls=%fused_computation.5 | convolution fusion | flops 3258972672 | bytes 55973888 | tf_op jit(solution)/shard_map/tgrd,kgd->grtk/dot_general | solution.py:24
  321.8 6.8 fusion.7
  328.7 23.4 %fusion.1 = f32[2,6,128]{2,1,0:T(8,128)S(1)} fusion(f32[2,8192,128,6]{2,1,3,0:T(8,128)} %get-tuple-element.11, f32[2,6,128]{2,1,0:T(8,128)S(1)} %get-tuple-element.8, pred[128,8192]{0,1:T(8,128)(4,1)S(1)} %fusion.11), kind=kLoop, calls=%fused_computation.6 | loop fusion | flops 62913024 | bytes 51392512 | tf_op jit(solution)/shard_map/reduce_sum | solution.py:36
  352.1 3.3 fusion.25
  355.4 26.0 %all-gather.13.cloned.1.call-done = bf16[1,8192,256]{2,1,0:T(8,128)(2,1)} async-done(((bf16[1,128,256]{2,1,0:T(8,128)(2,1)}), bf16[1,8192,256]{2,1,0:T(8,128)(2,1)}) %all-gather.13.cloned.1.call-update) | async-done | bytes 4194320 | tf_op jit(solution)/shard_map/all_gather | solution.py:87
  381.4 6.3 copy.89
  387.7 20.6 %fusion.36 = bf16[128,2,6,128]{0,3,2,1:T(8,128)(2,1)S(1)} fusion(f32[128,2,6,128]{0,3,2,1:T(8,128)} %fusion.25, bf16[8192,2,128,1]{0,2,3,1:T(8,128)(2,1)} %bitcast.169, f32[2,8192,128,6]{2,1,3,0:T(8,128)} %get-tuple-element.11, f32[2,6,128]{2,1,0:T(8,128)S(1)} %get-tuple-element.8, pred[128,8192]{0,1:T(8,128)(4,1)S(1)} %fusion.11, ...), kind=kOutput, calls=%fused_computation.37 | convolution fusion | flops 3284729856 | bytes 56766464 | tf_op jit(solution)/shard_map/grtk,kgd->grtd/dot_general | solution.py:37
  408.4 3.2 multiply_reduce_fusion.1
  415.1 4.6 scatter_custom_fusion
  420.1 113.8 %all_to_all.10 = bf16[64,1,24,1536]{3,2,1,0:T(8,128)(2,1)S(1)} all-to-all(bf16[64,1,24,1536]{3,2,1,0:T(8,128)(2,1)S(1)} %bitcast.162), channel_id=1, replica_groups=mesh['tok'=64,'grp'=4] {'tok'}, dimensions={0} | all-to-all | bytes 9437184 | tf_op jit(solution)/shard_map/all_to_all | solution.py:128
  536.1 4.0 convolution_maximum_fusion
  540.1 8.6 %convolution_convert_fusion = bf16[1536,1536]{1,0:T(8,128)(2,1)} fusion(bf16[1,384,1536]{2,1,0:T(8,128)(2,1)S(1)} %copy-done, f32[1536,384]{1,0:T(8,128)} %convolution_maximum_fusion, bf16[1536,1536]{1,0:T(8,128)(2,1)} %bitcast.167, bf16[1,1536,384]{2,1,0:T(8,128)(2,1)S(1)} %copy-done.11), kind=kOutput, calls=%fused_computation.15 | convolution fusion | flops 3627417600 | bytes 14155776 | tf_op jit(solution)/shard_map/dot_general | solution.py:138
  548.7 6.1 all-to-all-start.1
  555.3 3.8 gather_fusion.1
  559.5 102.9 %all-to-all-done.1 = bf16[64,1,24,1536]{3,2,1,0:T(8,128)(2,1)} async-done(((bf16[64,1,24,1536]{3,2,1,0:T(8,128)(2,1)}), bf16[64,1,24,1536]{3,2,1,0:T(8,128)(2,1)}, u32[]{:S(2)}, u32[]{:S(2)}) %all-to-all-start.1) | async-done | bytes 4718624 | tf_op jit(solution)/shard_map/all_to_all | solution.py:144
  662.4 3.0 bitcast_reduce_fusion.1
  665.4 2.8 convert_element_type.56
  668.2 6.9 gather_fusion
  675.1 4.9 reshape.263
  679.9 4.2 multiply_reduce_fusion
  (82 shorter events, 21.8 us)
Async XLA Ops:
  6.5 533.6 %copy-start = (bf16[1,384,1536]{2,1,0:T(8,128)(2,1)S(1)}, bf16[1,384,1536]{2,1,0:T(8,128)(2,1)}, u32[]{:S(2)}) copy-start(bf16[1,384,1536]{2,1,0:T(8,128)(2,1)} %param.27) | copy-start | bytes 3538948
  6.5 110.2 %all-gather.7.cloned.1.call-start = ((), (), s32[]{:S(2)}) async-start(), calls=%async_computation.2 | async-start | bytes 1052672 | tf_op jit(solution)/shard_map/all_gather | solution.py:79
  7.3 215.2 %all-gather.9.cloned.1.call-start = ((), (), s32[]{:S(2)}) async-start(), calls=%async_computation.3 | async-start | bytes 1052672 | tf_op jit(solution)/shard_map/all_gather | solution.py:80
  8.0 292.3 %all-gather.11.cloned.1.call-start = ((), (), s32[]{:S(2)}) async-start(), calls=%async_computation.4 | async-start | bytes 4259840 | tf_op jit(solution)/shard_map/all_gather | solution.py:86
  9.6 371.7 %all-gather.13.cloned.1.call-start = ((), (), s32[]{:S(2)}) async-start(), calls=%async_computation.5 | async-start | bytes 4259840 | tf_op jit(solution)/shard_map/all_gather | solution.py:87
  321.8 30.2 %slice-start = ((s8[12582912]{0:T(1024)(128)(4,1)}), s8[4194304]{0:T(1024)(128)(4,1)S(1)}, s32[]{:S(2)}) async-start(s8[12582912]{0:T(1024)(128)(4,1)} %bitcast.160), calls=%async_computation.6 | async-start | bytes 8388608
  328.6 23.4 %slice-start.1 = ((s8[12582912]{0:T(1024)(128)(4,1)}), s8[4194304]{0:T(1024)(128)(4,1)S(1)}, s32[]{:S(2)}) async-start(s8[12582912]{0:T(1024)(128)(4,1)} %bitcast.160), calls=%async_computation.7 | async-start | bytes 8388608
  328.7 23.4 %slice-start.2 = ((s8[12582912]{0:T(1024)(128)(4,1)}), s8[4194304]{0:T(1024)(128)(4,1)S(1)}, s32[]{:S(2)}) async-start(s8[12582912]{0:T(1024)(128)(4,1)} %bitcast.160), calls=%async_computation.8 | async-start | bytes 8388608
  387.7 20.6 %copy-start.6 = (f32[1,128,1536]{2,1,0:T(8,128)S(1)}, f32[1,128,1536]{2,1,0:T(8,128)}, u32[]{:S(2)}) copy-start(f32[1,128,1536]{2,1,0:T(8,128)} %param.14) | copy-start | bytes 2359300
  408.3 4.1 copy-start.9
  411.6 0.9 copy-start.1
  412.6 0.7 copy-start.4
  420.1 115.9 %copy-start.10 = (bf16[1,1536,384]{2,1,0:T(8,128)(2,1)S(1)}, bf16[1,1536,384]{2,1,0:T(8,128)(2,1)}, u32[]{:S(2)}) copy-start(bf16[1,1536,384]{2,1,0:T(8,128)(2,1)} %param.25) | copy-start | bytes 3538948
  533.9 2.2 copy-start.3
  536.1 4.0 copy-start.11
  548.7 6.1 copy-start.8
  548.7 6.4 copy-start.5
  548.7 6.4 copy-start.7
  548.7 113.7 %all-to-all-start.1 = ((bf16[64,1,24,1536]{3,2,1,0:T(8,128)(2,1)}), bf16[64,1,24,1536]{3,2,1,0:T(8,128)(2,1)}, u32[]{:S(2)}, u32[]{:S(2)}) async-start(bf16[64,1,24,1536]{3,2,1,0:T(8,128)(2,1)} %bitcast.165), calls=%async_computation.1 | async-start | bytes 9437184 | tf_op jit(solution)/shard_map/all_to_all | solution.py:144
  675.1 9.0 %copy-start.2 = (f32[128,1536]{1,0:T(8,128)S(1)}, f32[128,1536]{1,0:T(8,128)}, u32[]{:S(2)}) copy-start(f32[128,1536]{1,0:T(8,128)} %copy-done.1) | copy-start | bytes 2359300
Sparse Core Ops, SparseCore 0:
  11.1 105.6 all-gather.6
  120.5 101.9 all-gather.8
  225.1 75.1 all-gather.10
  303.0 78.3 all-gather.12
where the time goes:
time: 693 us; the launch traced here: 692 us
  waiting for transfers between devices  403 us (58%)
  blocking collectives  114 us (16%)
  matrix products  68.7 us (10%)
  other arithmetic  44.6 us (6%)
  local copies, waits for them, and re-layouts  41.6 us (6%)
  between operations  13.5 us (2%)
    all_to_all x1, blocking collectives, local(): lax.all_to_all(outgoing, 'tok', split_axis=0, concat_axis=0, tiled=True)  114 us
    all_to_all x1, waiting for transfers between devices, local(): lax.all_to_all(computed, 'tok', split_axis=0, concat_axis=0, tiled=True)  103 us
    all_gather x1, waiting for transfers between devices, local(): lax.all_gather(prefix_keys, ('tok', 'grp'), axis=0, tiled=True)  99.2 us
    all_gather x1, waiting for transfers between devices, local(): lax.all_gather(prefix_values, ('tok', 'grp'), axis=0, tiled=True)  96.9 us
    all_gather x1, waiting for transfers between devices, local(): lax.all_gather(own_keys, 'tok', axis=0, tiled=True)  76.4 us
    reduce_sum x2, other arithmetic, absorb(): denominator = denominator * factor + jnp.sum(weights, axis=-1)  30.2 us
    dot_general x2, matrix products, absorb(): jnp.einsum('tgrd,kgd->grtk', query_heads, key_heads, preferred_element_ty...  28.8 us
    all_gather x1, waiting for transfers between devices, local(): lax.all_gather(own_values, 'tok', axis=0, tiled=True)  26 us
  transfers between devices with their start and end apart: 5, of which 5 were waited for; matrix products, arithmetic and copies ran while one was open for 11% of the time, Pallas kernels for 0%

commit v1 on v0

v1 whole, which is shorter than its diff:
```python
import functools
import math

import jax
import jax.numpy as jnp
from jax import lax
from jax.experimental import pallas as pl
from jax.experimental.pallas import tpu as pltpu
from jax.sharding import Mesh, PartitionSpec as P

HEADS = 12
KVH = 2
HD = 128
REPEAT = HEADS // KVH
EXPERTS = 32
TOP = 4
CAP = 24
SLOTS = EXPERTS * CAP
ROWS = 128
KVW = KVH * HD
REACH = 34
CHUNK = 512
CHUNK_BLOCKS = CHUNK // ROWS
NEGATIVE = -1e30
SCALE = math.log2(math.e) / math.sqrt(HD)
F32 = jnp.float32
BF16 = jnp.bfloat16


def contract(left, right, left_dim, right_dim):
    return lax.dot_general(
        left, right, (((left_dim,), (right_dim,)), ((), ())), preferred_element_type=F32
    )


def attend_kernel(
    device_ref,
    inputs_ref,
    queries_ref,
    prefix_ref,
    suffix_ref,
    starts_ref,
    weight_hbm,
    gain_ref,
    router_ref,
    routes_ref,
    residual_ref,
    slots_ref,
    high_ref,
    low_ref,
    weight_ref,
    turned_ref,
    top_ref,
    total_ref,
    result_ref,
    weight_sem,
):
    weight_copy = pltpu.make_async_copy(weight_hbm, weight_ref, weight_sem)
    weight_copy.start()
    device = device_ref[0]
    width = REPEAT * ROWS
    for head in range(HEADS):
        group, place = head // REPEAT, head % REPEAT
        turned_ref[group, :, place * ROWS : (place + 1) * ROWS] = (
            queries_ref[:, head * HD : (head + 1) * HD].astype(F32).T.astype(BF16)
        )
    top_ref[...] = jnp.full_like(top_ref, NEGATIVE)
    total_ref[...] = jnp.zeros_like(total_ref)
    result_ref[...] = jnp.zeros_like(result_ref)

    def absorb(source, row, bias):
        for group in range(KVH):
            key_rows = source[pl.ds(row, CHUNK), group * HD : (group + 1) * HD]
            value_rows = source[pl.ds(row, CHUNK), KVW + group * HD : KVW + (group + 1) * HD]
            scores = contract(key_rows, turned_ref[group], 1, 0) * SCALE
            if bias is not None:
                scores = scores + jnp.concatenate([bias] * REPEAT, axis=1)
            old = top_ref[group]
            new = jnp.maximum(old, jnp.max(scores, axis=0, keepdims=True))
            factor = jnp.exp2(old - new)
            weights = jnp.exp2(scores - new)
            top_ref[group] = new
            total_ref[group] = total_ref[group] * factor + jnp.sum(weights, axis=0, keepdims=True)
            result_ref[group] = result_ref[group] * factor + contract(
                value_rows, weights.astype(BF16), 0, 0
            )

    def prefix_step(step, carry):
        absorb(prefix_ref, pl.multiple_of(step * CHUNK, CHUNK), None)
        return carry

    lax.fori_loop(0, prefix_ref.shape[0] // CHUNK, prefix_step, 0)

    positions = device * ROWS + lax.broadcasted_iota(jnp.int32, (1, ROWS), 1)
    starts = starts_ref[...]
    reached = jnp.minimum(device + 1, REACH)
    chunks = (reached + CHUNK_BLOCKS - 1) // CHUNK_BLOCKS
    first = jnp.maximum(device + 1 - chunks * CHUNK_BLOCKS, 0) * ROWS

    def suffix_step(step, carry):
        row = pl.multiple_of(first + step * CHUNK, ROWS)
        key_positions = row + lax.broadcasted_iota(jnp.int32, (CHUNK, ROWS), 0)
        valid = (key_positions >= starts) & (key_positions <= positions)
        absorb(suffix_ref, row, jnp.where(valid, 0.0, NEGATIVE))
        return carry

    lax.fori_loop(0, chunks, suffix_step, 0)

    weight_copy.wait()
    residual_ref[...] = inputs_ref[...]
    for group in range(KVH):
        attended = (result_ref[group] / total_ref[group]).T.astype(BF16)
        for place in range(REPEAT):
            head = group * REPEAT + place
            residual_ref[...] += jnp.dot(
                attended[place * ROWS : (place + 1) * ROWS],
                weight_ref[head * HD : (head + 1) * HD, :],
                preferred_element_type=F32,
            )
    residual = residual_ref[...]
    normed = (
        residual
        * lax.rsqrt(jnp.mean(residual * residual, axis=-1, keepdims=True) + 1e-06)
        * gain_ref[...]
    ).astype(BF16)

    expert_ids = lax.broadcasted_iota(jnp.int32, (EXPERTS, ROWS), 0)
    named = jnp.zeros((EXPERTS, ROWS), F32)
    for route in range(TOP):
        named = named + jnp.where(expert_ids == routes_ref[route : route + 1, :], 1.0, 0.0)
    earlier = (
        lax.broadcasted_iota(jnp.int32, (ROWS, ROWS), 0)
        < lax.broadcasted_iota(jnp.int32, (ROWS, ROWS), 1)
    )
    rank = jnp.dot(
        named.astype(BF16), jnp.where(earlier, 1.0, 0.0).astype(BF16), preferred_element_type=F32
    )
    rank = jnp.where(named > 0.5, rank, -1.0).astype(BF16)
    spread_row = lax.broadcasted_iota(jnp.int32, (SLOTS, EXPERTS), 0)
    spread_low = lax.broadcasted_iota(jnp.int32, (SLOTS, EXPERTS), 1) * CAP
    spread = jnp.where((spread_row >= spread_low) & (spread_row < spread_low + CAP), 1.0, 0.0).astype(
        BF16
    )
    slot_rank = jnp.dot(spread, rank, preferred_element_type=F32)
    slot_row = lax.broadcasted_iota(jnp.int32, (SLOTS, ROWS), 0)
    chosen = slot_rank == (slot_row % CAP).astype(F32)
    slots_ref[...] = jnp.dot(
        jnp.where(chosen, 1.0, 0.0).astype(BF16), normed, preferred_element_type=F32
    ).astype(BF16)

    logits = contract(router_ref[...], normed, 1, 1)
    sigmoids = named * jax.nn.sigmoid(logits)
    gates = sigmoids / jnp.sum(sigmoids, axis=0, keepdims=True)
    high = gates.astype(BF16)
    low = (gates - high.astype(F32)).astype(BF16)
    for part, part_ref in ((high, high_ref), (low, low_ref)):
        wide = jnp.dot(spread, part, preferred_element_type=F32)
        part_ref[...] = jnp.where(chosen, wide, 0.0).astype(BF16)


def attend(device, inputs, queries, prefix, suffix, starts, out_weight, gain, router, routes):
    rows, width = inputs.shape
    whole = pl.BlockSpec(memory_space=pltpu.VMEM)
    return pl.pallas_call(
        attend_kernel,
        out_shape=(
            jax.ShapeDtypeStruct((rows, width), F32),
            jax.ShapeDtypeStruct((SLOTS, width), BF16),
            jax.ShapeDtypeStruct((SLOTS, rows), BF16),
            jax.ShapeDtypeStruct((SLOTS, rows), BF16),
        ),
        in_specs=[
            pl.BlockSpec(memory_space=pltpu.SMEM),
            whole,
            whole,
            whole,
            whole,
            whole,
            pl.BlockSpec(memory_space=pl.ANY),
            whole,
            whole,
            whole,
        ],
        out_specs=(whole, whole, whole, whole),
        scratch_shapes=[
            pltpu.VMEM(out_weight.shape, BF16),
            pltpu.VMEM((KVH, HD, REPEAT * ROWS), BF16),
            pltpu.VMEM((KVH, 1, REPEAT * ROWS), F32),
            pltpu.VMEM((KVH, 1, REPEAT * ROWS), F32),
            pltpu.VMEM((KVH, HD, REPEAT * ROWS), F32),
            pltpu.SemaphoreType.DMA,
        ],
        compiler_params=pltpu.CompilerParams(vmem_limit_bytes=56 << 20),
        name="attend",
    )(device, inputs, queries, prefix, suffix, starts, out_weight, gain, router, routes)


def expert_kernel(rows_ref, gate_ref, up_ref, down_ref, out_ref, total_ref):
    step = pl.program_id(0)
    rows = rows_ref[...]
    gated = jax.nn.relu(jnp.dot(rows, gate_ref[0], preferred_element_type=F32))
    hidden = (gated * jnp.dot(rows, up_ref[0], preferred_element_type=F32)).astype(BF16)
    part = jnp.dot(hidden, down_ref[0], preferred_element_type=F32)

    @pl.when(step == 0)
    def _():
        total_ref[...] = part

    @pl.when(step > 0)
    def _():
        out_ref[...] = (total_ref[...] + part).astype(BF16)


def experts(rows, gate, up, down):
    count, width = rows.shape
    parts, _, hidden = gate.shape
    return pl.pallas_call(
        expert_kernel,
        grid=(parts,),
        out_shape=jax.ShapeDtypeStruct((count, width), BF16),
        in_specs=[
            pl.BlockSpec((count, width), lambda i: (0, 0)),
            pl.BlockSpec((1, width, hidden), lambda i: (i, 0, 0)),
            pl.BlockSpec((1, width, hidden), lambda i: (i, 0, 0)),
            pl.BlockSpec((1, hidden, width), lambda i: (i, 0, 0)),
        ],
        out_specs=pl.BlockSpec((count, width), lambda i: (0, 0)),
        scratch_shapes=[pltpu.VMEM((count, width), F32)],
        compiler_params=pltpu.CompilerParams(vmem_limit_bytes=48 << 20),
        name="experts",
    )(rows, gate, up, down)


def combine_kernel(residual_ref, high_ref, low_ref, results_ref, out_ref):
    results = results_ref[...]
    out_ref[...] = (
        residual_ref[...]
        + contract(high_ref[...], results, 0, 0)
        + contract(low_ref[...], results, 0, 0)
    )


def combine(residual, high, low, results):
    return pl.pallas_call(
        combine_kernel,
        out_shape=jax.ShapeDtypeStruct(residual.shape, F32),
        in_specs=[pl.BlockSpec(memory_space=pltpu.VMEM)] * 4,
        out_specs=pl.BlockSpec(memory_space=pltpu.VMEM),
        compiler_params=pltpu.CompilerParams(vmem_limit_bytes=32 << 20),
        name="combine",
    )(residual, high, low, results)


CHIPS = ("z", "x")
TOK = ("z", "x", "core")


def local(
    inputs,
    queries,
    keys,
    values,
    prefix_keys,
    prefix_values,
    lengths,
    out_weight,
    norm_gain,
    router_weight,
    routes,
    expert_gate,
    expert_up,
    expert_down,
):
    swap = [(0, 1), (1, 0)]
    gate = jnp.concatenate([expert_gate, lax.ppermute(expert_gate, "core", swap)])
    up = jnp.concatenate([expert_up, lax.ppermute(expert_up, "core", swap)])
    down = jnp.concatenate([expert_down, lax.ppermute(expert_down, "core", swap)])
    prefix = lax.all_gather(
        jnp.concatenate([prefix_keys, prefix_values], axis=1), TOK + ("grp",), axis=0, tiled=True
    )
    suffix = lax.all_gather(
        jnp.concatenate([keys[0], values[0]], axis=1), TOK, axis=0, tiled=True
    )
    device = lax.axis_index(TOK)
    positions = device * ROWS + jnp.arange(ROWS, dtype=jnp.int32)
    row_lengths = lax.dynamic_index_in_dim(lengths, lax.axis_index("grp"), 0, keepdims=False)
    request_ends = jnp.cumsum(row_lengths)
    starts = jnp.max(
        jnp.where(request_ends[None, :] <= positions[:, None], request_ends[None, :], 0), axis=1
    )
    residual, slots, high, low = attend(
        device.reshape(1).astype(jnp.int32),
        inputs[0],
        queries[0],
        prefix,
        suffix,
        starts.astype(jnp.int32)[None, :],
        out_weight,
        norm_gain[None, :],
        router_weight.T,
        routes[0].T,
    )
    width = inputs.shape[2]
    arrived = lax.all_to_all(
        slots.reshape(EXPERTS, CAP, width), CHIPS, split_axis=0, concat_axis=0, tiled=True
    )
    computed = experts(arrived.reshape(SLOTS, width), gate, up, down)
    returned = lax.all_to_all(
        computed.reshape(EXPERTS, CAP, width), CHIPS, split_axis=0, concat_axis=0, tiled=True
    )
    return combine(residual, high, low, returned.reshape(SLOTS, width))[None]


def solution(mesh):
    fine = Mesh(mesh.devices.reshape(8, 4, 2, 4), ("z", "x", "core", "grp"))
    placed = (
        P("grp", TOK, None),
        P("grp", TOK, None),
        P("grp", TOK, None),
        P("grp", TOK, None),
        P(TOK + ("grp",), None),
        P(TOK + ("grp",), None),
        P(),
        P(),
        P(),
        P(),
        P("grp", TOK, None),
        P(TOK, None, None),
        P(TOK, None, None),
        P(TOK, None, None),
    )
    return jax.shard_map(
        local, mesh=fine, in_specs=placed, out_specs=P("grp", TOK, None), check_vma=False
    )
```

time: 693 us -> 380 us (0.55)
  waiting for transfers between devices: 403 us -> 241 us
  matrix products: 68.7 us -> 0 us
  blocking collectives: 114 us -> 63.4 us
  local copies, waits for them, and re-layouts: 41.6 us -> 1.42 us
  other arithmetic: 44.6 us -> 8.64 us
  Pallas kernels: 0 us -> 29.9 us
  starting transfers between devices: 6.25 us -> 20.7 us
    all_gather x4 -> x2, waiting for transfers between devices: 298 us -> 191 us  [the longest x1 106 us: local(): lax.all_gather(jnp.concatenate([prefix_keys, prefix_values], axis=1), TOK...]
    dot_general x8 -> x0, matrix products: 68.7 us -> none  [the longest x2 28.8 us: absorb(): jnp.einsum('tgrd,kgd->grtk', query_heads, key_heads, preferred_element_ty...]
    all_to_all x1, waiting for transfers between devices: 103 us -> 48.1 us  [local(): lax.all_to_all(slots.reshape(EXPERTS, CAP, width), CHIPS, split_axis=0, c...]
    all_to_all x1, blocking collectives: 114 us -> 63.4 us  [local(): lax.all_to_all(computed.reshape(EXPERTS, CAP, width), CHIPS, split_axis=0...]
    reduce_sum x6 -> x0, other arithmetic: 37.5 us -> none  [the longest x2 30.2 us: absorb(): denominator = denominator * factor + jnp.sum(weights, axis=-1)]
    pallas_call x0 -> x3, Pallas kernels: none -> 29.9 us  [the longest x1 17.9 us: attend(): pl.pallas_call(attend_kernel, out_shape=(jax.ShapeDtypeStruct((rows, widt...]
    all_to_all x1, starting transfers between devices: 6.13 us -> 20 us  [local(): lax.all_to_all(slots.reshape(EXPERTS, CAP, width), CHIPS, split_axis=0, c...]
    gather x6 -> x0, local copies, waits for them, and re-layouts: 11 us -> none  [the longest x1 6.89 us: local(): expert_out[targets].reshape(tok_rows, TOP, model_width)]
  transfers between devices with their start and end apart: 5 -> 6, of which waited for: 5 -> 4; matrix products, arithmetic and copies ran while one was open for 11% -> 2% of each run, Pallas kernels for 0% -> 0%
where the time goes in v1:
time: 380 us; the launch traced here: 379 us
  waiting for transfers between devices  241 us (63%)
  blocking collectives  63.4 us (17%)
  Pallas kernels  29.9 us (8%)
  starting transfers between devices  20.7 us (5%)
  between operations  13.5 us (4%)
  other arithmetic  8.64 us (2%)
    all_gather x1, waiting for transfers between devices, local(): lax.all_gather(jnp.concatenate([prefix_keys, prefix_values], axis=1), TOK...  106 us
    all_gather x1, waiting for transfers between devices, local(): lax.all_gather(jnp.concatenate([keys[0], values[0]], axis=1), TOK, axis=0...  84.7 us
    all_to_all x1, blocking collectives, local(): lax.all_to_all(computed.reshape(EXPERTS, CAP, width), CHIPS, split_axis=0...  63.4 us
    all_to_all x1, waiting for transfers between devices, local(): lax.all_to_all(slots.reshape(EXPERTS, CAP, width), CHIPS, split_axis=0, c...  48.1 us
    all_to_all x1, starting transfers between devices, local(): lax.all_to_all(slots.reshape(EXPERTS, CAP, width), CHIPS, split_axis=0, c...  20 us
    pallas_call x1, Pallas kernels, attend(): pl.pallas_call(attend_kernel, out_shape=(jax.ShapeDtypeStruct((rows, widt...  17.9 us
    pallas_call x1, Pallas kernels, experts(): pl.pallas_call(expert_kernel, grid=(parts,), out_shape=jax.ShapeDtypeStru...  10.3 us
  transfers between devices with their start and end apart: 6, of which 4 were waited for; matrix products, arithmetic and copies ran while one was open for 2% of the time, Pallas kernels for 0%

profile of v1, /device:TPU:16, one launch (start us, length us, event | category | flops | bytes accessed | tf_op | source)
XLA Modules:
  0.0 379.1 jit_solution(18037946191202907422)
XLA Ops:
  6.5 1.3 pad_maximum_fusion.4
  7.8 0.0 all-gather.3.cloned.1.call-update
  7.9 0.0 all-gather.5.cloned.1.call-start
  7.9 1.5 pad_maximum_fusion.3
  9.5 0.0 all-gather.5.cloned.1.call-update
  9.5 1.3 broadcast_in_dim.24.gain_ref
  10.8 0.1 copy.17
  10.9 0.1 reduce
  11.1 0.7 select_reduce_fusion
  11.7 106.3 %all-gather.3.cloned.1.call-done.prefix_ref = bf16[2048,512]{1,0:T(8,128)(2,1)} async-done(((bf16[8,512]{1,0:T(8,128)(2,1)}), bf16[2048,512]{1,0:T(8,128)(2,1)}) %all-gather.3.cloned.1.call-update) | async-done | bytes 2097168 | tf_op jit(solution)/shard_map/all_gather | solution.py:278
  118.0 84.7 %all-gather.5.cloned.1.call-done.suffix_ref = bf16[8192,512]{1,0:T(8,128)(2,1)} async-done(((bf16[128,512]{1,0:T(8,128)(2,1)}), bf16[8192,512]{1,0:T(8,128)(2,1)}) %all-gather.5.cloned.1.call-update) | async-done | bytes 8388624 | tf_op jit(solution)/shard_map/all_gather | solution.py:281
  202.7 17.9 %attend.1 = (f32[128,1536]{1,0:T(8,128)}, bf16[768,1536]{1,0:T(8,128)(2,1)}, bf16[768,128]{1,0:T(8,128)(2,1)}, bf16[768,128]{1,0:T(8,128)(2,1)}) custom-call(s32[1]{0:T(128)} %bitcast.device_ref, f32[128,1536]{1,0:T(8,128)} %bitcast.21, bf16[128,1536]{1,0:T(8,128)(2,1)} %bitcast.22, bf16[2048,512]{1,0:T(8,128)(2,1)} %all-gather.3.cloned.1.call-done.prefix_ref, ...), custom_call_target="tpu_custom_call" | custom-call | tf_op jit(solution)/shard_map/attend/pallas_call | solution.py:164
  220.7 20.0 %all-to-all-start = ((bf16[32,24,1536]{2,1,0:T(8,128)(2,1)}), bf16[32,24,1536]{2,1,0:T(8,128)(2,1)S(1)}, u32[]{:S(2)}, u32[]{:S(2)}) async-start(bf16[32,24,1536]{2,1,0:T(8,128)(2,1)} %bitcast.20), calls=%async_computation | async-start | bytes 4718592 | tf_op jit(solution)/shard_map/all_to_all | solution.py:304
  240.7 0.1 collective-permute-start
  240.8 0.5 collective-permute-start.1
  241.3 0.1 collective-permute-start.2
  241.4 2.2 collective-permute-done
  243.6 1.7 pad_maximum_fusion.gate_ref
  245.3 1.7 pad_maximum_fusion.1.up_ref
  247.0 1.6 pad_maximum_fusion.2.down_ref
  248.6 48.1 %all-to-all-done = bf16[32,24,1536]{2,1,0:T(8,128)(2,1)S(1)} async-done(((bf16[32,24,1536]{2,1,0:T(8,128)(2,1)}), bf16[32,24,1536]{2,1,0:T(8,128)(2,1)S(1)}, u32[]{:S(2)}, u32[]{:S(2)}) %all-to-all-start) | async-done | bytes 2359328 | tf_op jit(solution)/shard_map/all_to_all | solution.py:304
  296.8 10.3 %experts.1 = bf16[768,1536]{1,0:T(8,128)(2,1)S(1)} custom-call(bf16[768,1536]{1,0:T(8,128)(2,1)S(1)} %bitcast.18, bf16[2,1536,384]{2,1,0:T(8,128)(2,1)} %pad_maximum_fusion.gate_ref, bf16[2,1536,384]{2,1,0:T(8,128)(2,1)} %pad_maximum_fusion.1.up_ref, bf16[2,384,1536]{2,1,0:T(8,128)(2,1)} %pad_maximum_fusion.2.down_ref), custom_call_target="tpu_custom_call" | custom-call | tf_op jit(solution)/shard_map/experts/pallas_call | solution.py:217
  307.2 63.4 %all_to_all.10 = bf16[32,24,1536]{2,1,0:T(8,128)(2,1)S(1)} all-to-all(bf16[32,24,1536]{2,1,0:T(8,128)(2,1)S(1)} %bitcast.19), channel_id=1, replica_groups=mesh['z'=8,'x'=4,'core'=2,'grp'=4] {'z','x'}, dimensions={0} | all-to-all | bytes 4718592 | tf_op jit(solution)/shard_map/all_to_all | solution.py:308
  370.6 1.7 combine.1
  (20 shorter events, 0.1 us)
Async XLA Ops:
  6.5 4.3 %copy-start = (s32[4,16]{1,0:T(4,128)S(1)}, s32[4,16]{1,0:T(4,128)}, u32[]{:S(2)}) copy-start(s32[4,16]{1,0:T(4,128)} %param.20) | copy-start | bytes 772
  6.5 111.4 %all-gather.3.cloned.1.call-start = ((), (), s32[]{:S(2)}) async-start(), calls=%async_computation.2 | async-start | bytes 2105344 | tf_op jit(solution)/shard_map/all_gather | solution.py:278
  7.9 194.9 %all-gather.5.cloned.1.call-start = ((), (), s32[]{:S(2)}) async-start(), calls=%async_computation.3 | async-start | bytes 8519680 | tf_op jit(solution)/shard_map/all_gather | solution.py:281
  220.7 20.0 %copy-start.4 = (bf16[1,1536,384]{2,1,0:T(8,128)(2,1)S(1)}, bf16[1,1536,384]{2,1,0:T(8,128)(2,1)}, u32[]{:S(2)}) copy-start(bf16[1,1536,384]{2,1,0:T(8,128)(2,1)} %param.25) | copy-start | bytes 3538948
  220.7 76.1 %all-to-all-start = ((bf16[32,24,1536]{2,1,0:T(8,128)(2,1)}), bf16[32,24,1536]{2,1,0:T(8,128)(2,1)S(1)}, u32[]{:S(2)}, u32[]{:S(2)}) async-start(bf16[32,24,1536]{2,1,0:T(8,128)(2,1)} %bitcast.20), calls=%async_computation | async-start | bytes 4718592 | tf_op jit(solution)/shard_map/all_to_all | solution.py:304
  240.7 4.6 %copy-start.5 = (bf16[1,1536,384]{2,1,0:T(8,128)(2,1)S(1)}, bf16[1,1536,384]{2,1,0:T(8,128)(2,1)}, u32[]{:S(2)}) copy-start(bf16[1,1536,384]{2,1,0:T(8,128)(2,1)} %param.26) | copy-start | bytes 3538948
  240.7 2.9 collective-permute-start
  240.8 4.5 %collective-permute-start.1 = (bf16[1,1536,384]{2,1,0:T(8,128)(2,1)}, bf16[1,1536,384]{2,1,0:T(8,128)(2,1)S(1)}, u32[]{:S(2)}, u32[]{:S(2)}) collective-permute-start(bf16[1,1536,384]{2,1,0:T(8,128)(2,1)} %param.26), channel_id=1, source_target_pairs={{0,4},{4,0},{1,5},{5,1},{2,6},{6,2},{3,7},{7,3},{8,12},{12,8},{9,1... | collective-permute-start | bytes 3538952 | tf_op jit(solution)/shard_map/ppermute | solution.py:276
  241.3 5.7 %collective-permute-start.2 = (bf16[1,384,1536]{2,1,0:T(8,128)(2,1)}, bf16[1,384,1536]{2,1,0:T(8,128)(2,1)S(1)}, u32[]{:S(2)}, u32[]{:S(2)}) collective-permute-start(bf16[1,384,1536]{2,1,0:T(8,128)(2,1)} %param.27), channel_id=1, source_target_pairs={{0,4},{4,0},{1,5},{5,1},{2,6},{6,2},{3,7},{7,3},{8,12},{12,8},{9,1... | collective-permute-start | bytes 3538952 | tf_op jit(solution)/shard_map/ppermute | solution.py:277
  245.3 1.7 copy-start.6
  307.1 63.5 %copy-start.1 = (f32[128,1536]{1,0:T(8,128)S(1)}, f32[128,1536]{1,0:T(8,128)}, u32[]{:S(2)}) copy-start(f32[128,1536]{1,0:T(8,128)} %get-tuple-element.9.residual_ref) | copy-start | bytes 2359300
  307.1 63.4 %copy-start.2 = (bf16[768,128]{1,0:T(8,128)(2,1)S(1)}, bf16[768,128]{1,0:T(8,128)(2,1)}, u32[]{:S(2)}) copy-start(bf16[768,128]{1,0:T(8,128)(2,1)} %get-tuple-element.10.high_ref) | copy-start | bytes 589828
  307.2 63.4 %copy-start.3 = (bf16[768,128]{1,0:T(8,128)(2,1)S(1)}, bf16[768,128]{1,0:T(8,128)(2,1)}, u32[]{:S(2)}) copy-start(bf16[768,128]{1,0:T(8,128)(2,1)} %get-tuple-element.11.low_ref) | copy-start | bytes 589828
Sparse Core Ops, SparseCore 0:
  11.1 106.8 all-gather.2
  120.7 81.9 all-gather.4

commit v2 on v1

v2 whole, which is shorter than its diff:
```python
import functools
import math

import jax
import jax.numpy as jnp
from jax import lax
from jax.experimental import pallas as pl
from jax.experimental.pallas import tpu as pltpu
from jax.sharding import Mesh, PartitionSpec as P

HEADS = 12
KVH = 2
HD = 128
REPEAT = HEADS // KVH
EXPERTS = 32
TOP = 4
CAP = 24
SLOTS = EXPERTS * CAP
ROWS = 128
KVW = KVH * HD
CHUNK = 512
NEGATIVE = -1e30
SCALE = math.log2(math.e) / math.sqrt(HD)
F32 = jnp.float32
BF16 = jnp.bfloat16


def contract(left, right, left_dim, right_dim):
    return lax.dot_general(
        left, right, (((left_dim,), (right_dim,)), ((), ())), preferred_element_type=F32
    )


Z, X, Y, CORES = 8, 4, 4, 2
PLANES = 5
SUB = 64
SUBS = CHUNK // SUB
PREFIX_CHUNKS = 2
SUFFIX_CHUNKS = CORES * PLANES
TICKS = CORES * (PLANES + PREFIX_CHUNKS)
EARLY = 6
MESH = pl.DeviceIdType.MESH


def attend_kernel(
    lengths_ref,
    inputs_hbm,
    queries_hbm,
    keys_hbm,
    values_hbm,
    prefix_keys_hbm,
    prefix_values_hbm,
    weight_hbm,
    gain_ref,
    router_ref,
    routes_ref,
    residual_ref,
    slots_ref,
    high_ref,
    low_ref,
    weight_ref,
    queries_ref,
    turned_ref,
    top_ref,
    total_ref,
    result_ref,
    held,
    corner,
    local_sem,
    z_send,
    z_recv,
    x_send,
    x_recv,
    half_send,
    half_recv,
    core_send,
    core_recv,
    pz_send,
    pz_recv,
    px_send,
    px_recv,
    py_send,
    py_recv,
    pc_send,
    pc_recv,
    corner_send,
    corner_recv,
):
    z, x = lax.axis_index("z"), lax.axis_index("x")
    core, y = lax.axis_index("core"), lax.axis_index("grp")
    device = (z * X + x) * CORES + core
    other = 1 - core
    right, left, across = lax.rem(x + 1, X), lax.rem(x + X - 1, X), lax.rem(x + 2, X)

    def chunk_of(which, plane):
        return which * PLANES + plane

    def block(plane, place):
        return held.at[chunk_of(core, plane), pl.ds(2 * place, 2)]

    def half(plane, place, kind):
        return held.at[chunk_of(core, plane), pl.ds(2 * place, 2), kind]

    def prefix_chunk(which, row):
        return SUFFIX_CHUNKS + which * PREFIX_CHUNKS + row // 2

    def prefix_sub(row, place):
        return lax.rem(row, 2) * X + place

    mine = prefix_chunk(core, y)
    loads = [
        pltpu.make_async_copy(keys_hbm, half(0, x, 0), local_sem.at[0]),
        pltpu.make_async_copy(values_hbm, half(0, x, 1), local_sem.at[1]),
        pltpu.make_async_copy(
            prefix_keys_hbm,
            held.at[mine, prefix_sub(y, x), 0, pl.ds(pl.multiple_of(z * 8, 8), 8)],
            local_sem.at[2],
        ),
        pltpu.make_async_copy(
            prefix_values_hbm,
            held.at[mine, prefix_sub(y, x), 1, pl.ds(pl.multiple_of(z * 8, 8), 8)],
            local_sem.at[3],
        ),
        pltpu.make_async_copy(queries_hbm, queries_ref, local_sem.at[4]),
        pltpu.make_async_copy(inputs_hbm, residual_ref, local_sem.at[5]),
        pltpu.make_async_copy(weight_hbm, weight_ref, local_sem.at[6]),
    ]
    for load in loads:
        load.start()

    barrier = pltpu.get_barrier_semaphore()
    for step in range(1, Z):
        pl.semaphore_signal(
            barrier, inc=1, device_id={"z": lax.rem(z + step, Z)}, device_id_type=MESH
        )
    for step in range(1, X):
        pl.semaphore_signal(
            barrier, inc=1, device_id={"x": lax.rem(x + step, X)}, device_id_type=MESH
        )
    for step in range(1, Y):
        pl.semaphore_signal(
            barrier, inc=1, device_id={"grp": lax.rem(y + step, Y)}, device_id_type=MESH
        )
    pl.semaphore_signal(barrier, inc=1, device_id={"core": other}, device_id_type=MESH)
    gives = (x == X - 1) & (core == 1)
    takes = (x == 0) & (core == 0)
    corner_to = {"z": lax.rem(z + PLANES, Z), "x": 0, "core": 0}
    corner_from = {"z": lax.rem(z + Z - PLANES, Z), "x": X - 1, "core": 1}

    @pl.when(gives)
    def _():
        pl.semaphore_signal(barrier, inc=1, device_id=corner_to, device_id_type=MESH)

    @pl.when(takes)
    def _():
        pl.semaphore_signal(barrier, inc=1, device_id=corner_from, device_id_type=MESH)

    greeted = (Z - 1) + (X - 1) + (Y - 1) + 1
    pl.semaphore_wait(barrier, greeted + jnp.where(gives | takes, 1, 0))

    def remote(source, target, send, recv, where):
        return pltpu.make_async_remote_copy(
            src_ref=source,
            dst_ref=target,
            send_sem=send,
            recv_sem=recv,
            device_id=where,
            device_id_type=MESH,
        )

    def z_copy(plane, place):
        return remote(
            block(plane - 1, place),
            block(plane, place),
            z_send.at[plane],
            z_recv.at[plane],
            {"z": lax.rem(z + 1, Z)},
        )

    def x_copy(plane, way, place):
        return remote(
            block(plane, place),
            block(plane, place),
            x_send.at[plane, way],
            x_recv.at[plane, way],
            {"x": right if way == 0 else left},
        )

    def half_copy(plane, way, place):
        return remote(
            half(plane, place, way),
            half(plane, place, way),
            half_send.at[plane, way],
            half_recv.at[plane, way],
            {"x": right if way == 0 else left},
        )

    def core_copy(plane, which):
        return remote(
            held.at[chunk_of(which, plane)],
            held.at[chunk_of(which, plane)],
            core_send.at[plane],
            core_recv.at[plane],
            {"core": other},
        )

    def pz_copy(step, place):
        region = held.at[mine, prefix_sub(y, x), :, pl.ds(pl.multiple_of(place * 8, 8), 8)]
        return remote(
            region, region, pz_send.at[step], pz_recv.at[step], {"z": lax.rem(z + step, Z)}
        )

    def px_copy(step, place):
        region = held.at[mine, prefix_sub(y, place)]
        return remote(
            region, region, px_send.at[step], px_recv.at[step], {"x": lax.rem(x + step, X)}
        )

    def py_copy(step, place):
        region = held.at[
            prefix_chunk(core, place), pl.ds(pl.multiple_of(lax.rem(place, 2) * X, X), X)
        ]
        return remote(
            region, region, py_send.at[step], py_recv.at[step], {"grp": lax.rem(y + step, Y)}
        )

    def pc_copy(which):
        region = held.at[pl.ds(SUFFIX_CHUNKS + which * PREFIX_CHUNKS, PREFIX_CHUNKS)]
        return remote(region, region, pc_send, pc_recv, {"core": other})

    corner_copy = remote(block(0, x), corner, corner_send, corner_recv, corner_to)

    def z_start(plane):
        z_copy(plane, x).start()

    def z_done(plane):
        z_copy(plane, x).wait_recv()

    def x_start(plane):
        for way in range(2):
            x_copy(plane, way, x).start()

    def x_turn(plane):
        for way, place in ((0, left), (1, right)):
            x_copy(plane, way, place).wait_recv()
            half_copy(plane, way, place).start()

    def core_start(plane):
        for way in range(2):
            half_copy(plane, way, across).wait_recv()
        core_copy(plane, core).start()

    def core_done(plane):
        core_copy(plane, other).wait_recv()

    def px_start():
        for step in range(1, Z):
            pz_copy(step, lax.rem(z + Z - step, Z)).wait_recv()
        for step in range(1, X):
            px_copy(step, x).start()

    def py_start():
        for step in range(1, X):
            px_copy(step, lax.rem(x + X - step, X)).wait_recv()
        for step in range(1, Y):
            py_copy(step, y).start()

    def pc_start():
        for step in range(1, Y):
            py_copy(step, lax.rem(y + Y - step, Y)).wait_recv()
        pc_copy(core).start()

    for load in loads[:2]:
        load.wait()
    z_start(1)
    x_start(0)
    for load in loads[2:4]:
        load.wait()
    for step in range(1, Z):
        pz_copy(step, z).start()

    @pl.when(gives)
    def _():
        corner_copy.start()

    loads[4].wait()
    for head in range(HEADS):
        group, place = head // REPEAT, head % REPEAT
        turned_ref[group, :, place * ROWS : (place + 1) * ROWS] = (
            queries_ref[:, head * HD : (head + 1) * HD].astype(F32).T.astype(BF16)
        )
    top_ref[...] = jnp.full_like(top_ref, NEGATIVE)
    total_ref[...] = jnp.zeros_like(total_ref)
    result_ref[...] = jnp.zeros_like(result_ref)
    positions = device * ROWS + lax.broadcasted_iota(jnp.int32, (1, ROWS), 1)
    starts = jnp.zeros((1, ROWS), jnp.int32)
    end = 0
    for request in range(lengths_ref.shape[1]):
        end = end + lengths_ref[y, request]
        starts = jnp.where(end <= positions, end, starts)

    def absorb(keys_of, values_of, bias):
        for group in range(KVH):
            key_rows, value_rows = keys_of(group), values_of(group)
            scores = contract(key_rows, turned_ref[group], 1, 0) * SCALE
            scores = scores + jnp.concatenate([bias] * REPEAT, axis=1)
            old = top_ref[group]
            new = jnp.maximum(old, jnp.max(scores, axis=0, keepdims=True))
            factor = jnp.exp2(old - new)
            weights = jnp.exp2(scores - new)
            top_ref[group] = new
            total_ref[group] = total_ref[group] * factor + jnp.sum(weights, axis=0, keepdims=True)
            result_ref[group] = result_ref[group] * factor + contract(
                value_rows, weights.astype(BF16), 0, 0
            )

    z_done(1)
    z_start(2)
    x_start(1)
    x_turn(0)
    px_start()
    core_start(0)

    actions = {
        1: [(core_done, 0), (z_done, 2), (z_start, 3), (x_start, 2), (x_turn, 1), (py_start,)],
        2: [(core_start, 1), (z_done, 3), (z_start, 4), (x_start, 3)],
        3: [(core_done, 1), (x_turn, 2)],
        4: [(core_start, 2), (z_done, 4), (x_start, 4)],
        5: [(core_done, 2), (x_turn, 3), (pc_start,)],
        6: [(core_start, 3)],
        7: [(x_turn, 4)],
        8: [(lambda: pc_copy(other).wait_recv(),), (core_start, 4)],
        10: [(core_done, 3)],
        13: [(core_done, 4)],
    }

    def act(tick):
        for action, *rest in actions[tick]:
            action(*rest)

    def tick_step(tick, carry):
        for known in actions:
            pl.when(tick == known)(functools.partial(act, known))
        late = tick >= EARLY + CORES * PREFIX_CHUNKS
        cached = (tick >= EARLY) & jnp.logical_not(late)
        counted = jnp.where(late, tick - CORES * PREFIX_CHUNKS, tick)
        plane = counted // CORES
        which = lax.rem(core + lax.rem(counted, CORES), CORES)
        cached_step = tick - EARLY
        cached_which = lax.rem(core + cached_step // PREFIX_CHUNKS, CORES)
        chunk = jnp.where(
            cached,
            SUFFIX_CHUNKS + cached_which * PREFIX_CHUNKS + lax.rem(cached_step + 2, PREFIX_CHUNKS),
            chunk_of(which, plane),
        )
        row = lax.broadcasted_iota(jnp.int32, (CHUNK, ROWS), 0)
        base = jnp.where(cached, 0, ((z - plane) * X * CORES + which) * ROWS)
        key_positions = base + row + (row - lax.rem(row, ROWS))
        low = jnp.where(cached, jnp.zeros_like(starts), starts)
        high = jnp.where(cached, jnp.full_like(positions, 1 << 20), positions)
        valid = (key_positions >= low) & (key_positions <= high)

        def part(kind):
            return lambda group: held[chunk, :, kind, :, group * HD : (group + 1) * HD].reshape(
                CHUNK, HD
            )

        absorb(part(0), part(1), jnp.where(valid, 0.0, NEGATIVE))
        return carry

    lax.fori_loop(0, TICKS, tick_step, 0)

    @pl.when(takes)
    def _():
        corner_copy.wait_recv()
        row = lax.broadcasted_iota(jnp.int32, (ROWS, ROWS), 0)
        key_positions = ((z - PLANES) * X * CORES + X * CORES - 1) * ROWS + row
        valid = (key_positions >= starts) & (key_positions <= positions)

        def part(kind):
            return lambda group: corner[:, kind, :, group * HD : (group + 1) * HD].reshape(ROWS, HD)

        absorb(part(0), part(1), jnp.where(valid, 0.0, NEGATIVE))

    for load in loads[5:]:
        load.wait()
    for group in range(KVH):
        attended = (result_ref[group] / total_ref[group]).T.astype(BF16)
        for place in range(REPEAT):
            head = group * REPEAT + place
            residual_ref[...] += jnp.dot(
                attended[place * ROWS : (place + 1) * ROWS],
                weight_ref[head * HD : (head + 1) * HD, :],
                preferred_element_type=F32,
            )
    residual = residual_ref[...]
    normed = (
        residual
        * lax.rsqrt(jnp.mean(residual * residual, axis=-1, keepdims=True) + 1e-06)
        * gain_ref[...]
    ).astype(BF16)

    expert_ids = lax.broadcasted_iota(jnp.int32, (EXPERTS, ROWS), 0)
    named = jnp.zeros((EXPERTS, ROWS), F32)
    for route in range(TOP):
        named = named + jnp.where(expert_ids == routes_ref[route : route + 1, :], 1.0, 0.0)
    earlier = (
        lax.broadcasted_iota(jnp.int32, (ROWS, ROWS), 0)
        < lax.broadcasted_iota(jnp.int32, (ROWS, ROWS), 1)
    )
    rank = jnp.dot(
        named.astype(BF16), jnp.where(earlier, 1.0, 0.0).astype(BF16), preferred_element_type=F32
    )
    rank = jnp.where(named > 0.5, rank, -1.0).astype(BF16)
    spread_row = lax.broadcasted_iota(jnp.int32, (SLOTS, EXPERTS), 0)
    spread_low = lax.broadcasted_iota(jnp.int32, (SLOTS, EXPERTS), 1) * CAP
    spread = jnp.where((spread_row >= spread_low) & (spread_row < spread_low + CAP), 1.0, 0.0).astype(
        BF16
    )
    slot_rank = jnp.dot(spread, rank, preferred_element_type=F32)
    slot_row = lax.broadcasted_iota(jnp.int32, (SLOTS, ROWS), 0)
    chosen = slot_rank == (slot_row % CAP).astype(F32)
    slots_ref[...] = jnp.dot(
        jnp.where(chosen, 1.0, 0.0).astype(BF16), normed, preferred_element_type=F32
    ).astype(BF16)

    logits = contract(router_ref[...], normed, 1, 1)
    sigmoids = named * jax.nn.sigmoid(logits)
    gates = sigmoids / jnp.sum(sigmoids, axis=0, keepdims=True)
    high = gates.astype(BF16)
    low = (gates - high.astype(F32)).astype(BF16)
    for part, part_ref in ((high, high_ref), (low, low_ref)):
        wide = jnp.dot(spread, part, preferred_element_type=F32)
        part_ref[...] = jnp.where(chosen, wide, 0.0).astype(BF16)

    for plane in range(1, PLANES):
        z_copy(plane, x).wait_send()
    for plane in range(PLANES):
        for way, place in ((0, left), (1, right)):
            x_copy(plane, way, x).wait_send()
            half_copy(plane, way, place).wait_send()
        core_copy(plane, core).wait_send()
    for step in range(1, Z):
        pz_copy(step, z).wait_send()
    for step in range(1, X):
        px_copy(step, x).wait_send()
    for step in range(1, Y):
        py_copy(step, y).wait_send()
    pc_copy(core).wait_send()

    @pl.when(gives)
    def _():
        corner_copy.wait_send()


def attend(
    lengths, inputs, queries, keys, values, prefix_keys, prefix_values, out_weight, gain, router, routes
):
    rows, width = inputs.shape
    whole = pl.BlockSpec(memory_space=pltpu.VMEM)
    apart = pl.BlockSpec(memory_space=pl.ANY)
    wires = pltpu.SemaphoreType.DMA
    pairs = [(PLANES,), (PLANES, 2), (PLANES, 2), (PLANES,), (Z,), (X,), (Y,), (), ()]
    return pl.pallas_call(
        attend_kernel,
        out_shape=(
            jax.ShapeDtypeStruct((rows, width), F32),
            jax.ShapeDtypeStruct((SLOTS, width), BF16),
            jax.ShapeDtypeStruct((SLOTS, rows), BF16),
            jax.ShapeDtypeStruct((SLOTS, rows), BF16),
        ),
        in_specs=[pl.BlockSpec(memory_space=pltpu.SMEM)] + [apart] * 7 + [whole] * 3,
        out_specs=(whole, whole, whole, whole),
        scratch_shapes=[
            pltpu.VMEM(out_weight.shape, BF16),
            pltpu.VMEM(queries.shape, BF16),
            pltpu.VMEM((KVH, HD, REPEAT * ROWS), BF16),
            pltpu.VMEM((KVH, 1, REPEAT * ROWS), F32),
            pltpu.VMEM((KVH, 1, REPEAT * ROWS), F32),
            pltpu.VMEM((KVH, HD, REPEAT * ROWS), F32),
            pltpu.VMEM((TICKS, SUBS, 2, SUB, KVW), BF16),
            pltpu.VMEM((ROWS // SUB, 2, SUB, KVW), BF16),
            wires((7,)),
        ]
        + [wires(shape) if shape else wires for shape in pairs for _ in range(2)],
        compiler_params=pltpu.CompilerParams(
            vmem_limit_bytes=56 << 20, collective_id=0, has_side_effects=True
        ),
        name="attend",
    )(
        lengths,
        inputs,
        queries,
        keys.reshape(ROWS // SUB, SUB, KVW),
        values.reshape(ROWS // SUB, SUB, KVW),
        prefix_keys,
        prefix_values,
        out_weight,
        gain,
        router,
        routes,
    )


def expert_kernel(rows_ref, *refs):
    out_ref = refs[-1]
    rows = rows_ref[...]
    total = None
    for gate_ref, up_ref, down_ref in (refs[0:3], refs[3:6]):
        gated = jax.nn.relu(jnp.dot(rows, gate_ref[0], preferred_element_type=F32))
        hidden = (gated * jnp.dot(rows, up_ref[0], preferred_element_type=F32)).astype(BF16)
        part = jnp.dot(hidden, down_ref[0], preferred_element_type=F32)
        total = part if total is None else total + part
    out_ref[...] = total.astype(BF16)


def experts(rows, *weights):
    count, width = rows.shape
    tile = 256
    held = [pl.BlockSpec(weight.shape, lambda i: (0, 0, 0)) for weight in weights]
    return pl.pallas_call(
        expert_kernel,
        grid=(count // tile,),
        out_shape=jax.ShapeDtypeStruct((count, width), BF16),
        in_specs=[pl.BlockSpec((tile, width), lambda i: (i, 0))] + held,
        out_specs=pl.BlockSpec((tile, width), lambda i: (i, 0)),
        compiler_params=pltpu.CompilerParams(vmem_limit_bytes=48 << 20),
        name="experts",
    )(rows, *weights)


def combine_kernel(residual_ref, high_ref, low_ref, results_ref, out_ref):
    results = results_ref[...]
    out_ref[...] = (
        residual_ref[...]
        + contract(high_ref[...], results, 0, 0)
        + contract(low_ref[...], results, 0, 0)
    )


def combine(residual, high, low, results):
    return pl.pallas_call(
        combine_kernel,
        out_shape=jax.ShapeDtypeStruct(residual.shape, F32),
        in_specs=[pl.BlockSpec(memory_space=pltpu.VMEM)] * 4,
        out_specs=pl.BlockSpec(memory_space=pltpu.VMEM),
        compiler_params=pltpu.CompilerParams(vmem_limit_bytes=32 << 20),
        name="combine",
    )(residual, high, low, results)


CHIPS = ("z", "x")
TOK = ("z", "x", "core")


def local(
    inputs,
    queries,
    keys,
    values,
    prefix_keys,
    prefix_values,
    lengths,
    out_weight,
    norm_gain,
    router_weight,
    routes,
    expert_gate,
    expert_up,
    expert_down,
):
    own = (expert_gate, expert_up, expert_down)
    partner = tuple(lax.ppermute(weight, "core", [(0, 1), (1, 0)]) for weight in own)
    residual, slots, high, low = attend(
        lengths,
        inputs[0],
        queries[0],
        keys[0],
        values[0],
        prefix_keys,
        prefix_values,
        out_weight,
        norm_gain[None, :],
        router_weight.T,
        routes[0].T,
    )
    width = inputs.shape[2]
    arrived = lax.all_to_all(
        slots.reshape(EXPERTS, CAP, width), CHIPS, split_axis=0, concat_axis=0, tiled=True
    )
    computed = experts(arrived.reshape(SLOTS, width), *own, *partner)
    returned = lax.all_to_all(
        computed.reshape(EXPERTS, CAP, width), CHIPS, split_axis=0, concat_axis=0, tiled=True
    )
    return combine(residual, high, low, returned.reshape(SLOTS, width))[None]


def solution(mesh):
    fine = Mesh(mesh.devices.reshape(8, 4, 2, 4), ("z", "x", "core", "grp"))
    placed = (
        P("grp", TOK, None),
        P("grp", TOK, None),
        P("grp", TOK, None),
        P("grp", TOK, None),
        P(TOK + ("grp",), None),
        P(TOK + ("grp",), None),
        P(),
        P(),
        P(),
        P(),
        P("grp", TOK, None),
        P(TOK, None, None),
        P(TOK, None, None),
        P(TOK, None, None),
    )
    return jax.shard_map(
        local, mesh=fine, in_specs=placed, out_specs=P("grp", TOK, None), check_vma=False
    )
```

time: 380 us -> 206 us (0.54)
  waiting for transfers between devices: 241 us -> 52.1 us
  Pallas kernels: 29.9 us -> 80.9 us
  starting transfers between devices: 20.7 us -> 5.76 us
  between operations: 13.5 us -> 0.08 us
  other arithmetic: 8.64 us -> 0 us
  local copies, waits for them, and re-layouts: 1.42 us -> 5.97 us
    all_gather x2 -> x0, waiting for transfers between devices: 191 us -> none  [the longest x1 106 us: local(): lax.all_gather(jnp.concatenate([prefix_keys, prefix_values], axis=1), TOK...]
    pallas_call x1, Pallas kernels: 17.9 us -> 68.7 us  [attend(): pl.pallas_call(attend_kernel, out_shape=(jax.ShapeDtypeStruct((rows, widt...]
    all_to_all x1, starting transfers between devices: 20 us -> 5.07 us  [local(): lax.all_to_all(slots.reshape(EXPERTS, CAP, width), CHIPS, split_axis=0, c...]
    concatenate x5 -> x0, other arithmetic: 7.82 us -> none  [the longest x1 1.67 us: local(): up = jnp.concatenate([expert_up, lax.ppermute(expert_up, 'core', swap)])]
    unnamed x14 -> x20, local copies, waits for them, and re-layouts: 0.04 us -> 4.67 us
  transfers between devices with their start and end apart: 6 -> 4, of which waited for: 4 -> 4; matrix products, arithmetic and copies ran while one was open for 2% -> 0% of each run, Pallas kernels for 0% -> 0%
where the time goes in v2:
time: 206 us
  Pallas kernels  80.9 us (39%)
  blocking collectives  61.1 us (30%)
  waiting for transfers between devices  52.1 us (25%)
  local copies, waits for them, and re-layouts  5.97 us (3%)
  starting transfers between devices  5.76 us (3%)
    pallas_call x1, Pallas kernels, attend(): pl.pallas_call(attend_kernel, out_shape=(jax.ShapeDtypeStruct((rows, widt...  68.7 us
    all_to_all x1, blocking collectives, local(): lax.all_to_all(computed.reshape(EXPERTS, CAP, width), CHIPS, split_axis=0...  61.1 us
    all_to_all x1, waiting for transfers between devices, local(): lax.all_to_all(slots.reshape(EXPERTS, CAP, width), CHIPS, split_axis=0, c...  48.5 us
    pallas_call x1, Pallas kernels, experts(): pl.pallas_call(expert_kernel, grid=(count // tile,), out_shape=jax.ShapeD...  10.5 us
    all_to_all x1, starting transfers between devices, local(): lax.all_to_all(slots.reshape(EXPERTS, CAP, width), CHIPS, split_axis=0, c...  5.07 us
    unnamed x20, local copies, waits for them, and re-layouts  4.67 us
  transfers between devices with their start and end apart: 4, of which 4 were waited for; matrix products, arithmetic and copies ran while one was open for 0% of the time, Pallas kernels for 0%

profile of v2, /device:TPU:16, one launch (start us, length us, event | category | flops | bytes accessed | tf_op | source)
XLA Modules:
  0.0 206.0 jit_solution(200400415195127213)
XLA Ops:
  0.0 1.3 broadcast_in_dim.6.gain_ref
  1.3 68.7 %attend.1 = (f32[128,1536]{1,0:T(8,128)}, bf16[768,1536]{1,0:T(8,128)(2,1)}, bf16[768,128]{1,0:T(8,128)(2,1)}, bf16[768,128]{1,0:T(8,128)(2,1)}) custom-call(s32[4,16]{1,0:T(4,128)} %lengths_ref.1, f32[128,1536]{1,0:T(8,128)} %bitcast.16, bf16[128,1536]{1,0:T(8,128)(2,1)} %bitcast.17, bf16[2,64,256]{2,1,0:T(8,128)(2,1)} %bitcast.19, ...), custom_call_target="tpu_custom_call" | custom-call | tf_op jit(solution)/shard_map/attend/pallas_call | solution.py:464
  70.1 0.0 copy-start
  70.1 0.0 copy-start.1
  70.1 0.0 copy-start.2
  70.1 5.1 %all-to-all-start = ((bf16[32,24,1536]{2,1,0:T(8,128)(2,1)}), bf16[32,24,1536]{2,1,0:T(8,128)(2,1)}, u32[]{:S(2)}, u32[]{:S(2)}) async-start(bf16[32,24,1536]{2,1,0:T(8,128)(2,1)} %bitcast.15), calls=%async_computation | async-start | bytes 4718592 | tf_op jit(solution)/shard_map/all_to_all | solution.py:588
  75.2 0.0 copy-done
  75.2 0.1 collective-permute-start
  75.3 0.0 copy-done.1
  75.3 0.5 collective-permute-start.1
  75.8 0.0 copy-done.2
  75.8 0.1 collective-permute-start.2
  75.9 2.2 %collective-permute-done.refs_3_ = bf16[1,1536,384]{2,1,0:T(8,128)(2,1)S(1)} collective-permute-done((bf16[1,1536,384]{2,1,0:T(8,128)(2,1)S(1)}, bf16[1,1536,384]{2,1,0:T(8,128)(2,1)S(1)}, u32[]{:S(2)}, u32[]{:S(2)}) %collective-permute-start) | collective-permute-done | bytes 1179680 | tf_op jit(solution)/shard_map/ppermute | solution.py:573
  78.1 1.1 copy-done.3
  79.2 0.6 collective-permute-done.1.refs_4_
  79.8 1.0 copy-done.5
  80.8 0.8 collective-permute-done.2.refs_5_
  81.6 48.5 %all-to-all-done = bf16[32,24,1536]{2,1,0:T(8,128)(2,1)} async-done(((bf16[32,24,1536]{2,1,0:T(8,128)(2,1)}), bf16[32,24,1536]{2,1,0:T(8,128)(2,1)}, u32[]{:S(2)}, u32[]{:S(2)}) %all-to-all-start) | async-done | bytes 2359328 | tf_op jit(solution)/shard_map/all_to_all | solution.py:588
  130.1 1.3 copy-done.4
  131.4 1.3 copy-done.6
  132.6 10.5 %experts.1 = bf16[768,1536]{1,0:T(8,128)(2,1)} custom-call(bf16[768,1536]{1,0:T(8,128)(2,1)} %bitcast.8.rows_ref, bf16[1,1536,384]{2,1,0:T(8,128)(2,1)S(1)} %copy-done, bf16[1,1536,384]{2,1,0:T(8,128)(2,1)S(1)} %copy-done.1, bf16[1,384,1536]{2,1,0:T(8,128)(2,1)S(1)} %copy-done.2, bf16[1,1536,384]{2,1,0:T(8,128)(2,1)S(1)} %copy-done.4, ...), custom_call_target="tpu_custom_call" | custom-call | tf_op jit(solution)/shard_map/experts/pallas_call | solution.py:521
  143.1 61.1 %all_to_all.10 = bf16[32,24,1536]{2,1,0:T(8,128)(2,1)S(1)} all-to-all(bf16[32,24,1536]{2,1,0:T(8,128)(2,1)} %bitcast.14), channel_id=1, replica_groups=mesh['z'=8,'x'=4,'core'=2,'grp'=4] {'z','x'}, dimensions={0} | all-to-all | bytes 4718592 | tf_op jit(solution)/shard_map/all_to_all | solution.py:592
  204.3 0.0 copy-done.7
  204.3 1.7 combine.1
  (9 shorter events, 0.0 us)
Async XLA Ops:
  70.1 5.1 %copy-start = (bf16[1,1536,384]{2,1,0:T(8,128)(2,1)S(1)}, bf16[1,1536,384]{2,1,0:T(8,128)(2,1)}, u32[]{:S(2)}) copy-start(bf16[1,1536,384]{2,1,0:T(8,128)(2,1)} %refs_0_.1) | copy-start | bytes 3538948
  70.1 5.2 %copy-start.1 = (bf16[1,1536,384]{2,1,0:T(8,128)(2,1)S(1)}, bf16[1,1536,384]{2,1,0:T(8,128)(2,1)}, u32[]{:S(2)}) copy-start(bf16[1,1536,384]{2,1,0:T(8,128)(2,1)} %refs_1_.1) | copy-start | bytes 3538948
  70.1 5.7 %copy-start.2 = (bf16[1,384,1536]{2,1,0:T(8,128)(2,1)S(1)}, bf16[1,384,1536]{2,1,0:T(8,128)(2,1)}, u32[]{:S(2)}) copy-start(bf16[1,384,1536]{2,1,0:T(8,128)(2,1)} %refs_2_.1) | copy-start | bytes 3538948
  70.1 60.0 %all-to-all-start = ((bf16[32,24,1536]{2,1,0:T(8,128)(2,1)}), bf16[32,24,1536]{2,1,0:T(8,128)(2,1)}, u32[]{:S(2)}, u32[]{:S(2)}) async-start(bf16[32,24,1536]{2,1,0:T(8,128)(2,1)} %bitcast.15), calls=%async_computation | async-start | bytes 4718592 | tf_op jit(solution)/shard_map/all_to_all | solution.py:588
  75.2 2.9 %collective-permute-start = (bf16[1,1536,384]{2,1,0:T(8,128)(2,1)S(1)}, bf16[1,1536,384]{2,1,0:T(8,128)(2,1)S(1)}, u32[]{:S(2)}, u32[]{:S(2)}) collective-permute-start(bf16[1,1536,384]{2,1,0:T(8,128)(2,1)S(1)} %copy-done), channel_id=1, source_target_pairs={{0,4},{4,0},{1,5},{5,1},{2,6},{6,2},{3,7},{7,3},{8,12},{12,8},{9,1... | collective-permute-start | bytes 3538952 | tf_op jit(solution)/shard_map/ppermute | solution.py:573
  75.3 4.5 %collective-permute-start.1 = (bf16[1,1536,384]{2,1,0:T(8,128)(2,1)S(1)}, bf16[1,1536,384]{2,1,0:T(8,128)(2,1)S(1)}, u32[]{:S(2)}, u32[]{:S(2)}) collective-permute-start(bf16[1,1536,384]{2,1,0:T(8,128)(2,1)S(1)} %copy-done.1), channel_id=1, source_target_pairs={{0,4},{4,0},{1,5},{5,1},{2,6},{6,2},{3,7},{7,3},{8,12},{12,8},{9,1... | collective-permute-start | bytes 3538952 | tf_op jit(solution)/shard_map/ppermute | solution.py:573
  75.8 5.8 %collective-permute-start.2 = (bf16[1,384,1536]{2,1,0:T(8,128)(2,1)S(1)}, bf16[1,384,1536]{2,1,0:T(8,128)(2,1)}, u32[]{:S(2)}, u32[]{:S(2)}) collective-permute-start(bf16[1,384,1536]{2,1,0:T(8,128)(2,1)S(1)} %copy-done.2), channel_id=1, source_target_pairs={{0,4},{4,0},{1,5},{5,1},{2,6},{6,2},{3,7},{7,3},{8,12},{12,8},{9,1... | collective-permute-start | bytes 3538952 | tf_op jit(solution)/shard_map/ppermute | solution.py:573
  78.1 1.1 copy-start.3
  79.8 1.0 copy-start.5
  130.1 1.3 copy-start.4
  131.3 1.3 copy-start.6
  143.1 61.1 %copy-start.7 = (f32[128,1536]{1,0:T(8,128)S(1)}, f32[128,1536]{1,0:T(8,128)}, u32[]{:S(2)}) copy-start(f32[128,1536]{1,0:T(8,128)} %get-tuple-element.9.residual_ref) | copy-start | bytes 2359300
  143.1 61.1 %copy-start.8 = (bf16[768,128]{1,0:T(8,128)(2,1)S(1)}, bf16[768,128]{1,0:T(8,128)(2,1)}, u32[]{:S(2)}) copy-start(bf16[768,128]{1,0:T(8,128)(2,1)} %get-tuple-element.10.high_ref) | copy-start | bytes 589828
  143.1 61.1 %copy-start.9 = (bf16[768,128]{1,0:T(8,128)(2,1)S(1)}, bf16[768,128]{1,0:T(8,128)(2,1)}, u32[]{:S(2)}) copy-start(bf16[768,128]{1,0:T(8,128)(2,1)} %get-tuple-element.11.low_ref) | copy-start | bytes 589828
